TPU v7x, 256 devices: a whole 4x4x8 slice. The times are simulated.
256 devices in a mesh: section: 16 (over x, y), tensor: 16 (over z, core).
Axes of the slice: x: 4, y: 4, z: 8, core: 2. Of those that a mesh axis runs over, the one named last changes fastest.
Arguments:
- queries: bfloat16 [16, 512, 8192], P('section', None, 'tensor'), may hold values from -20 to 20
- key_rows: bfloat16 [16, 512, 1024], P('section'), may hold values from -6 to 6
- value_rows: bfloat16 [16, 512, 1024], P('section'), may hold values from -6 to 6
- out_grad: bfloat16 [16, 512, 8192], P('section', None, 'tensor'), may hold values from -24 to 24
- layer_input: bfloat16 [16, 512, 8192], P('section', 'tensor'), may hold values from -64 to 64
- query_weight: bfloat16 [16, 8192, 8192], P('section', None, 'tensor'), may hold values from -0.0625 to 0.0625
- dion_basis: float32 [16, 8192, 256], P('section', 'tensor'), may hold values from -0.0625 to 0.0625
- lengths: int32 [16, 3], P('section'), may hold values from 1 to 256, 512 in all within a row
Outputs:
- upstream: bfloat16 [16, 512, 8192], P('section', 'tensor')
- left_factor: float32 [16, 8192, 256], P('section', 'tensor')
- right_factor: float32 [16, 8192, 256], P('section', 'tensor')
Inputs may be any that keep to these rules, and one draw needn't show every extreme that they name: For each section the lengths of the prompt, the chosen and the rejected response, in that order, summing to 512.
All inputs are finite; a program needn't handle non-finite values.
Results may differ from a plain program's by a relative error of at most 0.022.
Values may be sent and summed in bfloat16 or wider, within the bound.
No kernel may reach another device: no remote copies, remote signals or barrier semaphores. Data moves between devices by JAX's collectives and lax.ppermute only.
A program may use at most 64 MiB of HBM per device.

v0:
```python
import math
import jax
import jax.numpy as jnp
from jax import lax
from jax.sharding import PartitionSpec as P

D = 8192
HD = 128
GROUP = 8
rope_base = 500000.0
highest = lax.Precision.HIGHEST


def shifted(value, axis, steps):
    count = lax.axis_size(axis)
    first, last = (max(0, -steps), min(count, count - steps))
    return lax.ppermute(value, axis, [(source, source + steps) for source in range(first, last)])


def tree_layout(lengths_row, token_count):
    token_ids = jnp.arange(token_count, dtype=jnp.int32)
    bound_one = lengths_row[0]
    bound_two = lengths_row[0] + lengths_row[1]
    positions = jnp.where(token_ids < bound_two, token_ids, token_ids - lengths_row[1]).astype(
        jnp.float32
    )
    row_ids = token_ids[:, None]
    col_ids = token_ids[None, :]
    crossed = (row_ids >= bound_two) & (col_ids >= bound_one) & (col_ids < bound_two)
    visible = (col_ids <= row_ids) & jnp.logical_not(crossed)
    return (positions, visible)


def unrotate(rotated, positions):
    head_dim = rotated.shape[-1]
    half_dim = head_dim // 2
    freq_ids = jnp.arange(half_dim, dtype=jnp.float32)
    inverse = jnp.exp(-math.log(rope_base) * 2.0 * freq_ids / head_dim)
    angles = positions[:, None] * inverse[None, :]
    cosine = jnp.cos(angles)[:, None, :]
    sine_part = jnp.sin(angles)[:, None, :]
    first_half = rotated[..., :half_dim]
    second_half = rotated[..., half_dim:]
    return jnp.concatenate(
        [
            first_half * cosine + second_half * sine_part,
            second_half * cosine - first_half * sine_part,
        ],
        axis=-1,
    )


def local_backward(query_heads, grad_heads, key_block, value_block, visible):
    score_scale = 1.0 / math.sqrt(query_heads.shape[-1])
    scores = (
        jnp.einsum("qhd,kd->hqk", query_heads, key_block, preferred_element_type=jnp.float32)
        * score_scale
    )
    scores = jnp.where(visible[None], scores, -jnp.inf)
    row_max = jnp.max(scores, axis=-1, keepdims=True)
    exp_scores = jnp.exp(scores - row_max)
    weights = exp_scores / jnp.sum(exp_scores, axis=-1, keepdims=True)
    weights_low = weights.astype(jnp.bfloat16)
    outputs = jnp.einsum(
        "hqk,kd->qhd", weights_low, value_block, preferred_element_type=jnp.float32
    )
    out_dot = jnp.sum(grad_heads.astype(jnp.float32) * outputs, axis=-1)
    prob_grad = jnp.einsum(
        "qhd,kd->hqk", grad_heads, value_block, preferred_element_type=jnp.float32
    )
    score_grad = (weights * (prob_grad - out_dot.T[:, :, None])).astype(jnp.bfloat16)
    return (
        jnp.einsum("hqk,kd->qhd", score_grad, key_block, preferred_element_type=jnp.float32)
        * score_scale
    )


def local(queries, key_rows, value_rows, out_grad, layer_input, query_weight, dion_basis, lengths):
    token_count = queries.shape[1]
    local_width = queries.shape[2]
    local_heads = local_width // HD
    tensor_count = lax.axis_size("tensor")
    tensor_index = lax.axis_index("tensor")
    col_width = D // tensor_count
    gathered = lax.all_gather(layer_input[0], "tensor", axis=0, tiled=True)
    columns = lax.dynamic_slice_in_dim(gathered, tensor_index * col_width, col_width, 1)
    positions, visible = tree_layout(lengths[0], token_count)
    group_head = tensor_index * local_heads // GROUP
    key_block = lax.dynamic_slice_in_dim(key_rows[0], group_head * HD, HD, 1)
    value_block = lax.dynamic_slice_in_dim(value_rows[0], group_head * HD, HD, 1)
    rotated = local_backward(
        queries[0].reshape(token_count, local_heads, HD),
        out_grad[0].reshape(token_count, local_heads, HD),
        key_block,
        value_block,
        visible,
    )
    query_grad = unrotate(rotated, positions).reshape(token_count, local_width).astype(jnp.bfloat16)
    weight_local = query_weight[0]
    layer_grad = lax.psum_scatter(
        lax.dot_general(
            query_grad, weight_local, (((1,), (1,)), ((), ())), preferred_element_type=jnp.float32
        ).astype(jnp.bfloat16),
        "tensor",
        scatter_dimension=0,
        tiled=True,
    )
    upstream = shifted(layer_grad, "section", -1)
    grad_wide = query_grad.astype(jnp.float32)
    projected = lax.psum(jnp.dot(grad_wide, dion_basis[0], precision=highest), "tensor")
    column_wide = columns.astype(jnp.float32)
    left_raw = lax.dot_general(column_wide, projected, (((0,), (0,)), ((), ())), precision=highest)
    gram_part = lax.dot_general(left_raw, left_raw, (((0,), (0,)), ((), ())), precision=highest)
    mixed_part = jnp.dot(column_wide, left_raw, precision=highest)
    gram_total, mixed_total = lax.psum((gram_part, mixed_part), "tensor")
    lower_factor = jnp.linalg.cholesky(gram_total)
    left_orth = lax.linalg.triangular_solve(
        lower_factor, left_raw, left_side=False, lower=True, transpose_a=True
    )
    mixed_orth = lax.linalg.triangular_solve(
        lower_factor, mixed_total, left_side=False, lower=True, transpose_a=True
    )
    right_factor = lax.dot_general(
        grad_wide, mixed_orth, (((0,), (0,)), ((), ())), precision=highest
    )
    return (upstream[None], (left_orth * math.sqrt(D))[None], right_factor[None])


def solution(mesh):
    placed = (
        P("section", None, "tensor"),
        P("section", None, None),
        P("section", None, None),
        P("section", None, "tensor"),
        P("section", "tensor", None),
        P("section", None, "tensor"),
        P("section", "tensor", None),
        P("section", None),
    )
    return jax.shard_map(
        local,
        mesh=mesh,
        in_specs=placed,
        out_specs=(
            P("section", "tensor", None),
            P("section", "tensor", None),
            P("section", "tensor", None),
        ),
        check_vma=False,
    )
```

profile of v0, /device:TPU:26, one launch (start us, length us, event | category | flops | bytes accessed | tf_op | source)
XLA Modules:
  0.0 409.4 jit_solution(8106175779800506039)
XLA Ops:
  7.2 1.3 fusion.63
  8.6 0.6 iota_compare_fusion.5
  10.5 0.7 select_convert_fusion
  11.2 1.2 reshape_squeeze.6
  12.4 0.7 fusion.27
  13.4 2.1 fusion.64
  15.5 1.9 copy-done.3
  17.4 1.4 fusion.5
  18.8 0.4 copy.25
  19.2 1.2 reshape_squeeze.7
  20.4 0.6 fusion.13
  21.1 3.5 fusion.12
  24.6 0.5 multiply_cosine_fusion
  25.4 1.5 fusion.19
  27.0 0.7 all-gather.3.cloned.1.call-update
  27.7 111.7 %all-reduce.5.cloned.1.call-done = f32[512,256]{1,0:T(8,128)} async-done(((f32[512,256]{1,0:T(8,128)}), f32[512,256]{1,0:T(8,128)}) %all-reduce.5.cloned.1.call-update) | async-done | bytes 524304 | tf_op jit(solution)/shard_map/psum | solution.py:110
  139.4 58.2 %all-gather.3.cloned.1.call-done = bf16[1,512,8192]{2,1,0:T(8,128)(2,1)} async-done(((bf16[1,32,8192]{2,1,0:T(8,128)(2,1)}), bf16[1,512,8192]{2,1,0:T(8,128)(2,1)}) %all-gather.3.cloned.1.call-update) | async-done | bytes 8388624 | tf_op jit(solution)/shard_map/all_gather | solution.py:85
  197.7 1.9 fusion.23
  199.6 1.7 fusion.65
  201.3 2.5 fusion.21
  203.9 10.2 %convolution_convert_fusion = bf16[512,8192]{1,0:T(8,128)(2,1)} fusion(bf16[512,512]{0,1:T(8,128)(2,1)S(1)} %bitcast.114, bf16[1,8192,512]{2,1,0:T(8,128)(2,1)} %param.15), kind=kOutput, calls=%fused_computation.3 | convolution fusion | flops 4299161600 | bytes 17301504 | tf_op jit(solution)/shard_map/dot_general | solution.py:101
  214.1 99.1 %all-reduce.7.cloned.1.call-done = (f32[256,256]{0,1:T(8,128)}, f32[512,256]{1,0:T(8,128)}) async-done(((f32[256,256]{0,1:T(8,128)}, f32[512,256]{1,0:T(8,128)}), (f32[256,256]{0,1:T(8,128)}, f32[512,256]{1,0:T(8,128)})) %all-reduce.7.cloned.1.call-update) | async-done | bytes 786448 | tf_op jit(solution)/shard_map/psum | solution.py:115
  313.3 1.1 copy.22
  314.4 1.0 fusion.35
  315.4 11.7 %cholesky.50 = f32[128,128]{1,0:T(8,128)S(1)} custom-call(f32[128,128]{1,0:T(8,128)S(1)} %cholesky.118), custom_call_target="Cholesky" | custom-call | tf_op jit(solution)/shard_map/jit(cholesky)/cholesky | solution.py:116
  327.2 9.8 %custom-call.14 = f32[1,128,128]{1,2,0:T(8,128)S(1)} custom-call(f32[1,128,128]{2,1,0:T(8,128)S(1)} %get-tuple-element.43), custom_call_target="InvertDiagBlocksLowerTriangular" | custom-call | tf_op jit(solution)/shard_map/jit(cholesky)/cholesky | solution.py:116
  337.2 0.3 convolution_subtract_fusion.2
  337.5 11.7 %cholesky.105 = f32[128,128]{1,0:T(8,128)S(1)} custom-call(f32[128,128]{1,0:T(8,128)S(1)} %convolution_subtract_fusion.2), custom_call_target="Cholesky" | custom-call | tf_op jit(solution)/shard_map/jit(cholesky)/cholesky | solution.py:116
  349.2 0.6 compare_reduce_fusion
  349.9 0.6 compare_reduce_fusion.1
  351.9 4.0 while.4
  351.9 0.6 fusion.80
  352.5 1.4 bitcast_dynamic-update-slice_fusion.2
  353.9 0.6 fusion.80
  354.5 1.4 bitcast_dynamic-update-slice_fusion.2
  355.9 19.9 %custom-call.16 = f32[2,128,128]{1,2,0:T(8,128)S(1)} custom-call(f32[2,128,128]{2,1,0:T(8,128)S(1)} %get-tuple-element.18), custom_call_target="InvertDiagBlocksLowerTriangular" | custom-call | tf_op jit(solution)/shard_map/triangular_solve/custom-call.0 | solution.py:117
  375.8 0.4 fusion.33
  376.2 0.6 convolution_subtract_fusion.1
  376.8 0.4 fusion.50
  377.3 1.0 copy.23
  378.3 0.4 fusion.31
  378.8 8.2 %reduce-scatter.2.cloned.1.call-done = bf16[32,8192]{1,0:T(8,128)(2,1)} async-done(((bf16[512,8192]{1,0:T(8,128)(2,1)}), bf16[32,8192]{1,0:T(8,128)(2,1)}) %reduce-scatter.2.cloned.1.call-update) | async-done | bytes 524304 | tf_op jit(solution)/shard_map/reduce_scatter | solution.py:100
  387.0 2.8 collective-permute-start
  389.8 0.6 convolution_subtract_fusion
  390.4 0.4 fusion.49
  390.8 1.4 convolution_bitcast_fusion
  392.2 9.8 %collective-permute-done = bf16[32,8192]{1,0:T(8,128)(2,1)S(1)} collective-permute-done((bf16[32,8192]{1,0:T(8,128)(2,1)}, bf16[32,8192]{1,0:T(8,128)(2,1)S(1)}, u32[]{:S(2)}, u32[]{:S(2)}) %collective-permute-start) | collective-permute-done | bytes 524320 | tf_op jit(solution)/shard_map/ppermute | solution.py:17
  402.1 0.8 copy.50
  (32 shorter events, 1.3 us)
Async XLA Ops:
  7.2 5.2 %copy-start = (bf16[1,512,1024]{2,1,0:T(8,128)(2,1)S(1)}, bf16[1,512,1024]{2,1,0:T(8,128)(2,1)}, u32[]{:S(2)}) copy-start(bf16[1,512,1024]{2,1,0:T(8,128)(2,1)} %param.11) | copy-start | bytes 3145732
  7.2 132.2 %all-reduce.5.cloned.1.call-start = ((), (), s32[]{:S(2)}) async-start(), calls=%async_computation.2 | async-start | bytes 1048576 | tf_op jit(solution)/shard_map/psum | solution.py:110
  15.5 1.9 copy-start.3
  21.1 4.2 %copy-start.1 = (f32[1,512,256]{2,1,0:T(8,128)S(1)}, f32[1,512,256]{2,1,0:T(8,128)}, u32[]{:S(2)}) copy-start(f32[1,512,256]{2,1,0:T(8,128)} %param.16) | copy-start | bytes 1572868
  26.9 170.7 %all-gather.3.cloned.1.call-start = ((), (), s32[]{:S(2)}) async-start(), calls=%async_computation.3 | async-start | bytes 8912896 | tf_op jit(solution)/shard_map/all_gather | solution.py:85
  27.7 285.6 %all-reduce.7.cloned.1.call-start = ((), (), s32[]{:S(2)}) async-start(), calls=%async_computation.4 | async-start | bytes 1572864 | tf_op jit(solution)/shard_map/psum | solution.py:115
  203.8 183.2 %reduce-scatter.2.cloned.1.call-start = ((), (), s32[]{:S(2)}) async-start(), calls=%async_computation.1 | async-start | bytes 8912896 | tf_op jit(solution)/shard_map/reduce_scatter | solution.py:100
  313.3 65.1 %copy-start.2 = (f32[512,256]{1,0:T(8,128)S(1)}, f32[512,256]{1,0:T(8,128)}, u32[]{:S(2)}) copy-start(f32[512,256]{1,0:T(8,128)} %get-tuple-element.35) | copy-start | bytes 1572868
  387.0 15.1 %collective-permute-start = (bf16[32,8192]{1,0:T(8,128)(2,1)}, bf16[32,8192]{1,0:T(8,128)(2,1)S(1)}, u32[]{:S(2)}, u32[]{:S(2)}) collective-permute-start(bf16[32,8192]{1,0:T(8,128)(2,1)} %reduce-scatter.2.cloned.1.call-done), channel_id=1, source_target_pairs={{16,0},{32,16},{48,32},{64,48},{80,64},{96,80},{112,96},{128,112},... | collective-permute-start | bytes 1572872 | tf_op jit(solution)/shard_map/ppermute | solution.py:17
Sparse Core Ops, SparseCore 0:
  27.1 112.3 all-reduce.4
  141.4 56.2 all-gather.2
  203.9 109.2 all-reduce.6
  315.7 71.2 reduce-scatter.1
where the time goes:
time: 410 us; the launch traced here: 409 us
  waiting for transfers between devices  288 us (70%)
  other arithmetic  60.6 us (15%)
  matrix products  28.2 us (7%)
  between operations  16.7 us (4%)
  local copies, waits for them, and re-layouts  13.1 us (3%)
    psum x1, waiting for transfers between devices, local(): lax.psum(jnp.dot(grad_wide, dion_basis[0], precision=highest), 'tensor')  112 us
    psum x1, waiting for transfers between devices, local(): gram_total, mixed_total = lax.psum((gram_part, mixed_part), 'tensor')  99.1 us
    all_gather x1, waiting for transfers between devices, local(): gathered = lax.all_gather(layer_input[0], 'tensor', axis=0, tiled=True)  58.2 us
    another operation x7, other arithmetic, local(): lower_factor = jnp.linalg.cholesky(gram_total)  34.6 us
    another operation x4, other arithmetic, local(): lax.linalg.triangular_solve(lower_factor, left_raw, left_side=False, lowe...  19.9 us
    dot_general x1, matrix products, local(): lax.dot_general(query_grad, weight_local, (((1,), (1,)), ((), ())), prefe...  10.2 us
    ppermute x1, waiting for transfers between devices, shifted(): lax.ppermute(value, axis, [(source, source + steps) for source in range(f...  9.81 us
    reduce_scatter x1, waiting for transfers between devices, local(): lax.psum_scatter(lax.dot_general(query_grad, weight_local, (((1,), (1,)),...  8.25 us
  transfers between devices with their start and end apart: 5, of which 5 were waited for; matrix products, arithmetic and copies ran while one was open for 19% of the time, Pallas kernels for 0%

commit v1 on v0

--- a/solution.py
+++ b/solution.py
@@ -9,6 +9,27 @@
 GROUP = 8
 rope_base = 500000.0
 highest = lax.Precision.HIGHEST
+
+
+def collect(array, axis, dim):
+    length, mine, rows = (lax.axis_size(axis), lax.axis_index(axis), array.shape[dim])
+    upward = [(i, (i + 1) % length) for i in range(length)]
+    behind = [(i, (i - 1) % length) for i in range(length)]
+    result = jnp.zeros((*array.shape[:dim], length * rows, *array.shape[dim + 1 :]), array.dtype)
+    result = lax.dynamic_update_slice_in_dim(result, array, mine * rows, axis=dim)
+    from_left = from_right = array
+    half = length // 2
+    for turn in range(1, half + 1):
+        from_left = lax.ppermute(from_left, axis, upward)
+        result = lax.dynamic_update_slice_in_dim(
+            result, from_left, (mine - turn) % length * rows, axis=dim
+        )
+        if turn < length - half:
+            from_right = lax.ppermute(from_right, axis, behind)
+            result = lax.dynamic_update_slice_in_dim(
+                result, from_right, (mine + turn) % length * rows, axis=dim
+            )
+    return result
 
 
 def shifted(value, axis, steps):
@@ -82,7 +103,7 @@
     tensor_count = lax.axis_size("tensor")
     tensor_index = lax.axis_index("tensor")
     col_width = D // tensor_count
-    gathered = lax.all_gather(layer_input[0], "tensor", axis=0, tiled=True)
+    gathered = collect(layer_input[0], "tensor", 0)
     columns = lax.dynamic_slice_in_dim(gathered, tensor_index * col_width, col_width, 1)
     positions, visible = tree_layout(lengths[0], token_count)
     group_head = tensor_index * local_heads // GROUP

time: 410 us -> 358 us (0.87)
  waiting for transfers between devices: 288 us -> 190 us
  starting transfers between devices: 2.95 us -> 26.1 us
  local copies, waits for them, and re-layouts: 13.1 us -> 33.4 us
    psum x1, waiting for transfers between devices: 112 us -> 34 us  [local(): lax.psum(jnp.dot(grad_wide, dion_basis[0], precision=highest), 'tensor')]
    all_gather x1 -> x0, waiting for transfers between devices: 58.2 us -> none  [local(): gathered = lax.all_gather(layer_input[0], 'tensor', axis=0, tiled=True)]
    ppermute x0 -> x15, waiting for transfers between devices: none -> 39.4 us  [the longest x8 39.4 us: collect(): from_left = lax.ppermute(from_left, axis, upward)]
    ppermute x0 -> x15, starting transfers between devices: none -> 23.1 us  [the longest x7 23 us: collect(): from_right = lax.ppermute(from_right, axis, behind)]
    dynamic_update_slice x0 -> x16, local copies, waits for them, and re-layouts: none -> 15.5 us  [the longest x8 7.73 us: collect(): lax.dynamic_update_slice_in_dim(result, from_left, (mine - turn) % length...]
    broadcast_in_dim x0 -> x1, local copies, waits for them, and re-layouts: none -> 4.24 us  [collect(): jnp.zeros((*array.shape[:dim], length * rows, *array.shape[dim + 1:]), ar...]
  transfers between devices with their start and end apart: 5 -> 19, of which waited for: 5 -> 11; matrix products, arithmetic and copies ran while one was open for 19% -> 32% of each run, Pallas kernels for 0% -> 0%
where the time goes in v1:
time: 358 us; the launch traced here: 357 us
  waiting for transfers between devices  190 us (53%)
  other arithmetic  61.2 us (17%)
  local copies, waits for them, and re-layouts  33.4 us (9%)
  matrix products  29.2 us (8%)
  starting transfers between devices  26.1 us (7%)
  between operations  16.7 us (5%)
    psum x1, waiting for transfers between devices, local(): gram_total, mixed_total = lax.psum((gram_part, mixed_part), 'tensor')  101 us
    ppermute x8, waiting for transfers between devices, collect(): from_left = lax.ppermute(from_left, axis, upward)  39.4 us
    another operation x7, other arithmetic, local(): lower_factor = jnp.linalg.cholesky(gram_total)  34.6 us
    psum x1, waiting for transfers between devices, local(): lax.psum(jnp.dot(grad_wide, dion_basis[0], precision=highest), 'tensor')  34 us
    ppermute x7, starting transfers between devices, collect(): from_right = lax.ppermute(from_right, axis, behind)  23 us
    another operation x4, other arithmetic, local(): lax.linalg.triangular_solve(lower_factor, left_raw, left_side=False, lowe...  20.5 us
    dot_general x1, matrix products, local(): lax.dot_general(query_grad, weight_local, (((1,), (1,)), ((), ())), prefe...  10.2 us
    ppermute x1, waiting for transfers between devices, shifted(): lax.ppermute(value, axis, [(source, source + steps) for source in range(f...  9.87 us
  transfers between devices with their start and end apart: 19, of which 11 were waited for; matrix products, arithmetic and copies ran while one was open for 32% of the time, Pallas kernels for 0%

profile of v1, /device:TPU:26, one launch (start us, length us, event | category | flops | bytes accessed | tf_op | source)
XLA Modules:
  0.0 357.0 jit_solution(9803714601794097048)
XLA Ops:
  7.3 5.3 %collective-permute-start.2 = (bf16[32,8192]{1,0:T(8,128)(2,1)}, bf16[32,8192]{1,0:T(8,128)(2,1)}, u32[]{:S(2)}, u32[]{:S(2)}) collective-permute-start(bf16[32,8192]{1,0:T(8,128)(2,1)} %bitcast.116), channel_id=1, source_target_pairs={{0,15},{1,0},{2,1},{3,2},{4,3},{5,4},{6,5},{7,6},{8,7},{9,8},{10,9... | collective-permute-start | bytes 1572872 | tf_op jit(solution)/shard_map/ppermute | solution.py:28
  12.6 1.3 fusion.63
  16.5 1.2 reshape_squeeze.6
  18.7 2.1 fusion.64
  20.8 1.9 copy-done.5
  22.8 1.4 fusion.5
  24.6 1.2 reshape_squeeze.7
  26.5 3.5 fusion.12
  30.7 1.5 fusion.19
  32.3 4.2 %broadcast_in_dim.39 = bf16[512,8192]{1,0:T(8,128)(2,1)} broadcast(bf16[]{:T(256)} %constant.196.clone.1), dimensions={} | broadcast | bytes 8388610 | tf_op jit(solution)/shard_map/broadcast_in_dim | solution.py:18
  37.4 3.0 collective-permute-start.4
  40.4 1.9 constant_dynamic-update-slice_fusion.15
  42.3 1.9 constant_dynamic-update-slice_fusion.14
  44.1 3.5 collective-permute-done.3
  47.6 3.0 collective-permute-start.6
  51.4 0.9 constant_dynamic-update-slice_fusion.12
  52.3 5.5 %collective-permute-done.5 = bf16[32,8192]{1,0:T(8,128)(2,1)S(1)} collective-permute-done((bf16[32,8192]{1,0:T(8,128)(2,1)S(1)}, bf16[32,8192]{1,0:T(8,128)(2,1)S(1)}, u32[]{:S(2)}, u32[]{:S(2)}) %collective-permute-start.5) | collective-permute-done | bytes 524320 | tf_op jit(solution)/shard_map/ppermute | solution.py:23
  57.8 3.0 collective-permute-start.8
  62.4 5.6 %collective-permute-done.7 = bf16[32,8192]{1,0:T(8,128)(2,1)S(1)} collective-permute-done((bf16[32,8192]{1,0:T(8,128)(2,1)S(1)}, bf16[32,8192]{1,0:T(8,128)(2,1)S(1)}, u32[]{:S(2)}, u32[]{:S(2)}) %collective-permute-start.7) | collective-permute-done | bytes 524320 | tf_op jit(solution)/shard_map/ppermute | solution.py:23
  68.0 3.0 collective-permute-start.10
  72.6 5.5 %collective-permute-done.9 = bf16[32,8192]{1,0:T(8,128)(2,1)S(1)} collective-permute-done((bf16[32,8192]{1,0:T(8,128)(2,1)S(1)}, bf16[32,8192]{1,0:T(8,128)(2,1)S(1)}, u32[]{:S(2)}, u32[]{:S(2)}) %collective-permute-start.9) | collective-permute-done | bytes 524320 | tf_op jit(solution)/shard_map/ppermute | solution.py:23
  78.1 3.0 collective-permute-start.12
  82.8 5.6 %collective-permute-done.11 = bf16[32,8192]{1,0:T(8,128)(2,1)S(1)} collective-permute-done((bf16[32,8192]{1,0:T(8,128)(2,1)S(1)}, bf16[32,8192]{1,0:T(8,128)(2,1)S(1)}, u32[]{:S(2)}, u32[]{:S(2)}) %collective-permute-start.11) | collective-permute-done | bytes 524320 | tf_op jit(solution)/shard_map/ppermute | solution.py:23
  88.3 3.0 collective-permute-start.14
  91.3 0.9 constant_dynamic-update-slice_fusion.5
  93.0 5.1 %collective-permute-done.13 = bf16[32,8192]{1,0:T(8,128)(2,1)S(1)} collective-permute-done((bf16[32,8192]{1,0:T(8,128)(2,1)S(1)}, bf16[32,8192]{1,0:T(8,128)(2,1)S(1)}, u32[]{:S(2)}, u32[]{:S(2)}) %collective-permute-start.13) | collective-permute-done | bytes 524320 | tf_op jit(solution)/shard_map/ppermute | solution.py:23
  99.8 8.6 %collective-permute-done.15 = bf16[32,8192]{1,0:T(8,128)(2,1)S(1)} collective-permute-done((bf16[32,8192]{1,0:T(8,128)(2,1)S(1)}, bf16[32,8192]{1,0:T(8,128)(2,1)S(1)}, u32[]{:S(2)}, u32[]{:S(2)}) %collective-permute-start.15) | collective-permute-done | bytes 524320 | tf_op jit(solution)/shard_map/ppermute | solution.py:23
  109.2 34.0 %all-reduce.5.cloned.1.call-done = f32[512,256]{1,0:T(8,128)} async-done(((f32[512,256]{1,0:T(8,128)}), f32[512,256]{1,0:T(8,128)}) %all-reduce.5.cloned.1.call-update) | async-done | bytes 524304 | tf_op jit(solution)/shard_map/psum | solution.py:131
  143.2 1.9 fusion.27
  145.2 2.5 fusion.25
  147.7 1.7 fusion.65
  149.6 10.2 %convolution_convert_fusion = bf16[512,8192]{1,0:T(8,128)(2,1)} fusion(bf16[512,512]{0,1:T(8,128)(2,1)S(1)} %bitcast.109, bf16[1,8192,512]{2,1,0:T(8,128)(2,1)} %param.15), kind=kOutput, calls=%fused_computation.3 | convolution fusion | flops 4299161600 | bytes 17301504 | tf_op jit(solution)/shard_map/dot_general | solution.py:122
  159.9 100.9 %all-reduce.7.cloned.1.call-done = (f32[256,256]{0,1:T(8,128)}, f32[512,256]{1,0:T(8,128)}) async-done(((f32[256,256]{0,1:T(8,128)}, f32[512,256]{1,0:T(8,128)}), (f32[256,256]{0,1:T(8,128)}, f32[512,256]{1,0:T(8,128)})) %all-reduce.7.cloned.1.call-update) | async-done | bytes 786448 | tf_op jit(solution)/shard_map/psum | solution.py:136
  260.8 1.1 copy.22
  262.0 1.0 fusion.35
  263.0 11.7 %cholesky.50 = f32[128,128]{1,0:T(8,128)S(1)} custom-call(f32[128,128]{1,0:T(8,128)S(1)} %cholesky.118), custom_call_target="Cholesky" | custom-call | tf_op jit(solution)/shard_map/jit(cholesky)/cholesky | solution.py:137
  274.7 9.8 %custom-call.14 = f32[1,128,128]{1,2,0:T(8,128)S(1)} custom-call(f32[1,128,128]{2,1,0:T(8,128)S(1)} %get-tuple-element.43), custom_call_target="InvertDiagBlocksLowerTriangular" | custom-call | tf_op jit(solution)/shard_map/jit(cholesky)/cholesky | solution.py:137
  285.0 11.7 %cholesky.105 = f32[128,128]{1,0:T(8,128)S(1)} custom-call(f32[128,128]{1,0:T(8,128)S(1)} %convolution_subtract_fusion), custom_call_target="Cholesky" | custom-call | tf_op jit(solution)/shard_map/jit(cholesky)/cholesky | solution.py:137
  299.5 4.0 %while.4 = (s32[]{:T(128)}, f32[256,256]{1,0:T(8,128)S(1)}, s32[2,2]{1,0:T(2,128)S(1)}, f32[2,128,128]{2,1,0:T(8,128)S(1)}, s32[]{:T(128)}) while((s32[]{:T(128)}, f32[256,256]{1,0:T(8,128)S(1)}, s32[2,2]{1,0:T(2,128)S(1)}, f32[2,128,128]{2,1,0:T(8,128)S(1)}, s32[]{:T(128)}) %tuple.38), condition=%wide.while_cond, body=%wide.while_body.sunk | while | flops 2 | bytes 131181 | solution.py:138
  300.1 1.4 bitcast_dynamic-update-slice_fusion.2
  302.1 1.4 bitcast_dynamic-update-slice_fusion.2
  304.1 20.5 %custom-call.16 = f32[2,128,128]{1,2,0:T(8,128)S(1)} custom-call(f32[2,128,128]{2,1,0:T(8,128)} %copy-done.4), custom_call_target="InvertDiagBlocksLowerTriangular" | custom-call | tf_op jit(solution)/shard_map/triangular_solve/custom-call.0 | solution.py:138
  326.1 1.0 copy.23
  327.1 1.4 fusion.30
  328.5 6.0 %reduce-scatter.2.cloned.1.call-done = bf16[32,8192]{1,0:T(8,128)(2,1)} async-done(((bf16[512,8192]{1,0:T(8,128)(2,1)}), bf16[32,8192]{1,0:T(8,128)(2,1)}) %reduce-scatter.2.cloned.1.call-update) | async-done | bytes 524304 | tf_op jit(solution)/shard_map/reduce_scatter | solution.py:121
  334.6 2.7 collective-permute-start
  338.3 1.4 convolution_bitcast_fusion
  339.8 9.9 %collective-permute-done = bf16[32,8192]{1,0:T(8,128)(2,1)S(1)} collective-permute-done((bf16[32,8192]{1,0:T(8,128)(2,1)}, bf16[32,8192]{1,0:T(8,128)(2,1)S(1)}, u32[]{:S(2)}, u32[]{:S(2)}) %collective-permute-start) | collective-permute-done | bytes 524320 | tf_op jit(solution)/shard_map/ppermute | solution.py:38
  (80 shorter events, 21.6 us)
Async XLA Ops:
  7.2 10.5 %copy-start = (bf16[1,512,1024]{2,1,0:T(8,128)(2,1)S(1)}, bf16[1,512,1024]{2,1,0:T(8,128)(2,1)}, u32[]{:S(2)}) copy-start(bf16[1,512,1024]{2,1,0:T(8,128)(2,1)} %param.11) | copy-start | bytes 3145732
  7.2 136.1 %all-reduce.5.cloned.1.call-start = ((), (), s32[]{:S(2)}) async-start(), calls=%async_computation.2 | async-start | bytes 1048576 | tf_op jit(solution)/shard_map/psum | solution.py:131
  7.2 30.2 %collective-permute-start.1 = (bf16[32,8192]{1,0:T(8,128)(2,1)}, bf16[32,8192]{1,0:T(8,128)(2,1)}, u32[]{:S(2)}, u32[]{:S(2)}) collective-permute-start(bf16[32,8192]{1,0:T(8,128)(2,1)} %bitcast.115), channel_id=1, source_target_pairs={{0,1},{1,2},{2,3},{3,4},{4,5},{5,6},{6,7},{7,8},{8,9},{9,10},{10,1... | collective-permute-start | bytes 1572872 | tf_op jit(solution)/shard_map/ppermute | solution.py:23
  7.3 30.2 %collective-permute-start.2 = (bf16[32,8192]{1,0:T(8,128)(2,1)}, bf16[32,8192]{1,0:T(8,128)(2,1)}, u32[]{:S(2)}, u32[]{:S(2)}) collective-permute-start(bf16[32,8192]{1,0:T(8,128)(2,1)} %bitcast.116), channel_id=1, source_target_pairs={{0,15},{1,0},{2,1},{3,2},{4,3},{5,4},{6,5},{7,6},{8,7},{9,8},{10,9... | collective-permute-start | bytes 1572872 | tf_op jit(solution)/shard_map/ppermute | solution.py:28
  20.8 1.9 copy-start.5
  26.5 4.3 %copy-start.1 = (f32[1,512,256]{2,1,0:T(8,128)S(1)}, f32[1,512,256]{2,1,0:T(8,128)}, u32[]{:S(2)}) copy-start(f32[1,512,256]{2,1,0:T(8,128)} %param.16) | copy-start | bytes 1572868
  29.9 6.6 %copy-start.3 = (bf16[1,32,8192]{2,1,0:T(8,128)(2,1)S(1)}, bf16[1,32,8192]{2,1,0:T(8,128)(2,1)}, u32[]{:S(2)}) copy-start(bf16[1,32,8192]{2,1,0:T(8,128)(2,1)} %param.14) | copy-start | bytes 1572868
  32.3 228.5 %all-reduce.7.cloned.1.call-start = ((), (), s32[]{:S(2)}) async-start(), calls=%async_computation.3 | async-start | bytes 1572864 | tf_op jit(solution)/shard_map/psum | solution.py:136
  37.4 10.2 %collective-permute-start.3 = (bf16[32,8192]{1,0:T(8,128)(2,1)}, bf16[32,8192]{1,0:T(8,128)(2,1)S(1)}, u32[]{:S(2)}, u32[]{:S(2)}) collective-permute-start(bf16[32,8192]{1,0:T(8,128)(2,1)} %collective-permute-done.1), channel_id=1, source_target_pairs={{0,1},{1,2},{2,3},{3,4},{4,5},{5,6},{6,7},{7,8},{8,9},{9,10},{10,1... | collective-permute-start | bytes 1572872 | tf_op jit(solution)/shard_map/ppermute | solution.py:23
  37.4 10.2 %collective-permute-start.4 = (bf16[32,8192]{1,0:T(8,128)(2,1)}, bf16[32,8192]{1,0:T(8,128)(2,1)S(1)}, u32[]{:S(2)}, u32[]{:S(2)}) collective-permute-start(bf16[32,8192]{1,0:T(8,128)(2,1)} %collective-permute-done.2), channel_id=1, source_target_pairs={{0,15},{1,0},{2,1},{3,2},{4,3},{5,4},{6,5},{7,6},{8,7},{9,8},{10,9... | collective-permute-start | bytes 1572872 | tf_op jit(solution)/shard_map/ppermute | solution.py:28
  47.6 10.2 %collective-permute-start.5 = (bf16[32,8192]{1,0:T(8,128)(2,1)S(1)}, bf16[32,8192]{1,0:T(8,128)(2,1)S(1)}, u32[]{:S(2)}, u32[]{:S(2)}) collective-permute-start(bf16[32,8192]{1,0:T(8,128)(2,1)S(1)} %collective-permute-done.3), channel_id=1, source_target_pairs={{0,1},{1,2},{2,3},{3,4},{4,5},{5,6},{6,7},{7,8},{8,9},{9,10},{10,1... | collective-permute-start | bytes 1572872 | tf_op jit(solution)/shard_map/ppermute | solution.py:23
  47.6 10.2 %collective-permute-start.6 = (bf16[32,8192]{1,0:T(8,128)(2,1)S(1)}, bf16[32,8192]{1,0:T(8,128)(2,1)S(1)}, u32[]{:S(2)}, u32[]{:S(2)}) collective-permute-start(bf16[32,8192]{1,0:T(8,128)(2,1)S(1)} %collective-permute-done.4), channel_id=1, source_target_pairs={{0,15},{1,0},{2,1},{3,2},{4,3},{5,4},{6,5},{7,6},{8,7},{9,8},{10,9... | collective-permute-start | bytes 1572872 | tf_op jit(solution)/shard_map/ppermute | solution.py:28
  57.8 10.2 %collective-permute-start.7 = (bf16[32,8192]{1,0:T(8,128)(2,1)S(1)}, bf16[32,8192]{1,0:T(8,128)(2,1)S(1)}, u32[]{:S(2)}, u32[]{:S(2)}) collective-permute-start(bf16[32,8192]{1,0:T(8,128)(2,1)S(1)} %collective-permute-done.5), channel_id=1, source_target_pairs={{0,1},{1,2},{2,3},{3,4},{4,5},{5,6},{6,7},{7,8},{8,9},{9,10},{10,1... | collective-permute-start | bytes 1572872 | tf_op jit(solution)/shard_map/ppermute | solution.py:23
  57.8 10.2 %collective-permute-start.8 = (bf16[32,8192]{1,0:T(8,128)(2,1)S(1)}, bf16[32,8192]{1,0:T(8,128)(2,1)S(1)}, u32[]{:S(2)}, u32[]{:S(2)}) collective-permute-start(bf16[32,8192]{1,0:T(8,128)(2,1)S(1)} %collective-permute-done.6), channel_id=1, source_target_pairs={{0,15},{1,0},{2,1},{3,2},{4,3},{5,4},{6,5},{7,6},{8,7},{9,8},{10,9... | collective-permute-start | bytes 1572872 | tf_op jit(solution)/shard_map/ppermute | solution.py:28
  68.0 10.2 %collective-permute-start.9 = (bf16[32,8192]{1,0:T(8,128)(2,1)S(1)}, bf16[32,8192]{1,0:T(8,128)(2,1)S(1)}, u32[]{:S(2)}, u32[]{:S(2)}) collective-permute-start(bf16[32,8192]{1,0:T(8,128)(2,1)S(1)} %collective-permute-done.7), channel_id=1, source_target_pairs={{0,1},{1,2},{2,3},{3,4},{4,5},{5,6},{6,7},{7,8},{8,9},{9,10},{10,1... | collective-permute-start | bytes 1572872 | tf_op jit(solution)/shard_map/ppermute | solution.py:23
  68.0 10.2 %collective-permute-start.10 = (bf16[32,8192]{1,0:T(8,128)(2,1)S(1)}, bf16[32,8192]{1,0:T(8,128)(2,1)S(1)}, u32[]{:S(2)}, u32[]{:S(2)}) collective-permute-start(bf16[32,8192]{1,0:T(8,128)(2,1)S(1)} %collective-permute-done.8), channel_id=1, source_target_pairs={{0,15},{1,0},{2,1},{3,2},{4,3},{5,4},{6,5},{7,6},{8,7},{9,8},{10,9... | collective-permute-start | bytes 1572872 | tf_op jit(solution)/shard_map/ppermute | solution.py:28
  78.1 10.2 %collective-permute-start.11 = (bf16[32,8192]{1,0:T(8,128)(2,1)S(1)}, bf16[32,8192]{1,0:T(8,128)(2,1)S(1)}, u32[]{:S(2)}, u32[]{:S(2)}) collective-permute-start(bf16[32,8192]{1,0:T(8,128)(2,1)S(1)} %collective-permute-done.9), channel_id=1, source_target_pairs={{0,1},{1,2},{2,3},{3,4},{4,5},{5,6},{6,7},{7,8},{8,9},{9,10},{10,1... | collective-permute-start | bytes 1572872 | tf_op jit(solution)/shard_map/ppermute | solution.py:23
  78.1 10.2 %collective-permute-start.12 = (bf16[32,8192]{1,0:T(8,128)(2,1)S(1)}, bf16[32,8192]{1,0:T(8,128)(2,1)S(1)}, u32[]{:S(2)}, u32[]{:S(2)}) collective-permute-start(bf16[32,8192]{1,0:T(8,128)(2,1)S(1)} %collective-permute-done.10), channel_id=1, source_target_pairs={{0,15},{1,0},{2,1},{3,2},{4,3},{5,4},{6,5},{7,6},{8,7},{9,8},{10,9... | collective-permute-start | bytes 1572872 | tf_op jit(solution)/shard_map/ppermute | solution.py:28
  88.3 9.8 %collective-permute-start.13 = (bf16[32,8192]{1,0:T(8,128)(2,1)S(1)}, bf16[32,8192]{1,0:T(8,128)(2,1)S(1)}, u32[]{:S(2)}, u32[]{:S(2)}) collective-permute-start(bf16[32,8192]{1,0:T(8,128)(2,1)S(1)} %collective-permute-done.11), channel_id=1, source_target_pairs={{0,1},{1,2},{2,3},{3,4},{4,5},{5,6},{6,7},{7,8},{8,9},{9,10},{10,1... | collective-permute-start | bytes 1572872 | tf_op jit(solution)/shard_map/ppermute | solution.py:23
  88.3 10.6 %collective-permute-start.14 = (bf16[32,8192]{1,0:T(8,128)(2,1)S(1)}, bf16[32,8192]{1,0:T(8,128)(2,1)S(1)}, u32[]{:S(2)}, u32[]{:S(2)}) collective-permute-start(bf16[32,8192]{1,0:T(8,128)(2,1)S(1)} %collective-permute-done.12), channel_id=1, source_target_pairs={{0,15},{1,0},{2,1},{3,2},{4,3},{5,4},{6,5},{7,6},{8,7},{9,8},{10,9... | collective-permute-start | bytes 1572872 | tf_op jit(solution)/shard_map/ppermute | solution.py:28
  98.1 10.2 %collective-permute-start.15 = (bf16[32,8192]{1,0:T(8,128)(2,1)S(1)}, bf16[32,8192]{1,0:T(8,128)(2,1)S(1)}, u32[]{:S(2)}, u32[]{:S(2)}) collective-permute-start(bf16[32,8192]{1,0:T(8,128)(2,1)S(1)} %collective-permute-done.13), channel_id=1, source_target_pairs={{0,1},{1,2},{2,3},{3,4},{4,5},{5,6},{6,7},{7,8},{8,9},{9,10},{10,1... | collective-permute-start | bytes 1572872 | tf_op jit(solution)/shard_map/ppermute | solution.py:23
  149.4 185.2 %reduce-scatter.2.cloned.1.call-start = ((), (), s32[]{:S(2)}) async-start(), calls=%async_computation.1 | async-start | bytes 8912896 | tf_op jit(solution)/shard_map/reduce_scatter | solution.py:121
  260.8 77.1 %copy-start.2 = (f32[512,256]{1,0:T(8,128)S(1)}, f32[512,256]{1,0:T(8,128)}, u32[]{:S(2)}) copy-start(f32[512,256]{1,0:T(8,128)} %get-tuple-element.35) | copy-start | bytes 1572868
  303.5 0.7 copy-start.4
  334.6 15.1 %collective-permute-start = (bf16[32,8192]{1,0:T(8,128)(2,1)}, bf16[32,8192]{1,0:T(8,128)(2,1)S(1)}, u32[]{:S(2)}, u32[]{:S(2)}) collective-permute-start(bf16[32,8192]{1,0:T(8,128)(2,1)} %reduce-scatter.2.cloned.1.call-done), channel_id=1, source_target_pairs={{16,0},{32,16},{48,32},{64,48},{80,64},{96,80},{112,96},{128,112},... | collective-permute-start | bytes 1572872 | tf_op jit(solution)/shard_map/ppermute | solution.py:38
Sparse Core Ops, SparseCore 0:
  32.4 110.7 all-reduce.4
  149.5 111.2 all-reduce.6
  263.4 71.1 reduce-scatter.1
